TPU v7x, 128 devices: a whole 4x4x4 slice. The times are simulated.
128 devices in a mesh: row: 8 (over x, core), col: 16 (over z, y).
Axes of the slice: x: 4, y: 4, z: 4, core: 2. Of those that a mesh axis runs over, the one named last changes fastest.
Arguments:
- model_init: float32 [2, 2, 16, 16384], P(None, None, None, 'col'), may hold values from -2 to 2
- observed: float32 [2, 2, 16, 32768], P(None, None, None, ('row', 'col')), may hold values from -6 to 6
- left_bases: bfloat16 [128, 64, 2, 96, 2, 256], P(('row', 'col')), may hold values from -0.078125 to 0.078125
- right_bases: bfloat16 [128, 64, 2, 96, 2, 256], P('row', 'col'), may hold values from -0.078125 to 0.078125
- tile_ranks: int32 [128, 64, 2], P('row', 'col'), may hold values from 8 to 96
- gate_start: int32 [16, 32768], P(None, ('row', 'col')), may hold values from 0 to 31
- gate_stop: int32 [16, 32768], P(None, ('row', 'col')), may hold values from 32 to 64
Outputs:
- model_final: float32 [2, 2, 16, 16384], P(None, None, None, 'col')
- residual_final: float32 [2, 2, 16, 32768], P(None, None, None, ('row', 'col'))
All inputs are finite; a program needn't handle non-finite values.
Results may differ from a plain program's by a relative error of at most 0.009.
Values may be sent and summed in bfloat16 or wider, within the bound.
No kernel may reach another device: no remote copies, remote signals or barrier semaphores. Data moves between devices by JAX's collectives and lax.ppermute only.
A program may use at most 128 MiB of HBM per device.

v0:
```python
import math
import jax
import jax.numpy as jnp
from jax import lax
from jax.sharding import PartitionSpec as P

NV = 16
TILE = 256
RMAX = 96
F = 2
NT = 64
ITERS = 2
step_length = 0.8


def time_table(samples):
    sample_times = jnp.arange(samples, dtype=jnp.float32)[:, None]
    freq_bins = (3.0 + 5.0 * jnp.arange(F, dtype=jnp.float32))[None, :]
    phases = 2.0 * math.pi * sample_times * freq_bins / samples
    return jnp.concatenate([jnp.cos(phases), -jnp.sin(phases)], axis=1)


def apply_gate(field, gate_start, gate_stop):
    transform = time_table(NT)
    flattened = field.reshape(2 * F, -1)
    signal = jnp.dot(transform, flattened, precision=lax.Precision.HIGHEST)
    sample_index = jnp.arange(NT, dtype=jnp.int32)[:, None, None]
    window = ((sample_index >= gate_start[None]) & (sample_index < gate_stop[None])).astype(
        jnp.float32
    )
    windowed = signal * window.reshape(NT, -1)
    returned = jnp.dot(transform.T, windowed, precision=lax.Precision.HIGHEST) * (2.0 / NT)
    return returned.reshape(field.shape)


def pair_rows(field):
    real_part, imag_part = (field[0], field[1])
    upper_pair = jnp.stack([real_part, imag_part], axis=3)
    lower_pair = jnp.stack([imag_part, -real_part], axis=3)
    joined = jnp.stack([upper_pair, lower_pair], axis=1)
    return jnp.transpose(joined, (3, 0, 1, 2, 4, 5))


def combine(stacked):
    real_part = stacked[:, :, 0, :, 0] - stacked[:, :, 1, :, 1]
    imag_part = stacked[:, :, 0, :, 1] + stacked[:, :, 1, :, 0]
    joined = jnp.stack([real_part, imag_part], axis=0)
    joined = jnp.transpose(joined, (0, 2, 3, 1, 4))
    return joined.reshape(joined.shape[0], joined.shape[1], joined.shape[2], -1)


def forward(low_model, left_bases, right_bases, rank_keep):
    blocks = low_model.shape[3] // TILE
    paired = pair_rows(low_model.reshape(2, F, NV, blocks, TILE))
    coefficients = jnp.einsum(
        "jfavcs,ijfkcs->ijfavk", paired, right_bases, preferred_element_type=jnp.float32
    )
    coefficients = (coefficients * rank_keep[:, :, :, None, None, :]).astype(jnp.bfloat16)
    sendable = coefficients.reshape(coefficients.shape[0], coefficients.shape[1], F, 2, NV * RMAX)
    received = lax.all_to_all(sendable, "col", split_axis=0, concat_axis=1, tiled=True)
    received = received.reshape(received.shape[0], received.shape[1], F, 2, NV, RMAX)
    modeled = jnp.einsum(
        "ijfavk,ijfkcn->ifavcn", received, left_bases, preferred_element_type=jnp.float32
    )
    return combine(modeled)


def adjoint(residual, left_bases, right_bases, rank_keep):
    blocks = residual.shape[3] // TILE
    paired = pair_rows(residual.astype(jnp.bfloat16).reshape(2, F, NV, blocks, TILE))
    coefficients = jnp.einsum(
        "ifavcn,ijfkcn->ijfavk", paired, left_bases, preferred_element_type=jnp.float32
    )
    coefficients = coefficients.astype(jnp.bfloat16)
    sendable = coefficients.reshape(blocks, coefficients.shape[1], F, 2, NV * RMAX)
    received = lax.all_to_all(sendable, "col", split_axis=1, concat_axis=0, tiled=True)
    received = received.reshape(received.shape[0], received.shape[1], F, 2, NV, RMAX)
    received = received * rank_keep[:, :, :, None, None, :].astype(jnp.bfloat16)
    column_terms = jnp.einsum(
        "ijfavk,ijfkcs->jfavcs", received, right_bases, preferred_element_type=jnp.float32
    )
    return combine(column_terms)


def shards(model_init, observed, left_bases, right_bases, tile_ranks, gate_start, gate_stop):
    rank_index = jnp.arange(RMAX, dtype=jnp.int32)
    rank_keep = (rank_index < tile_ranks[..., None]).astype(jnp.float32)
    estimate = model_init
    low_model = model_init.astype(jnp.bfloat16)
    for iteration in range(ITERS):
        predicted = forward(low_model, left_bases, right_bases, rank_keep)
        residual = apply_gate(predicted - observed, gate_start, gate_stop)
        grad_local = adjoint(residual, left_bases, right_bases, rank_keep)
        gradient = lax.psum(grad_local.astype(jnp.bfloat16), "row").astype(jnp.float32)
        estimate = estimate - step_length * gradient
        low_model = estimate.astype(jnp.bfloat16)
    predicted = forward(low_model, left_bases, right_bases, rank_keep)
    residual = apply_gate(predicted - observed, gate_start, gate_stop)
    return (estimate, residual)


def solution(mesh):
    placed = (
        P(None, None, None, "col"),
        P(None, None, None, ("row", "col")),
        P(("row", "col"), None, None, None, None, None),
        P("row", "col", None, None, None, None),
        P("row", "col", None),
        P(None, ("row", "col")),
        P(None, ("row", "col")),
    )
    return jax.shard_map(
        shards,
        mesh=mesh,
        in_specs=placed,
        out_specs=(P(None, None, None, "col"), P(None, None, None, ("row", "col"))),
        check_vma=False,
    )
```

profile of v0, /device:TPU:6, one launch (start us, length us, event | category | flops | bytes accessed | tf_op | source)
XLA Modules:
  0.0 333.3 jit_solution(16784469923808730853)
XLA Ops:
  9.1 9.1 %fusion.24 = bf16[16,4,2,2,16,96]{5,4,0,3,2,1:T(8,128)(2,1)S(1)} fusion(bf16[16,4,2,96,2,256,1]{5,4,3,2,1,0,6:T(2,128)(2,1)} %bitcast.384, f32[16,4,2,96]{3,0,2,1:T(8,128)S(1)} %get-tuple-element.31, bf16[2,1,16,4,2,256]{5,2,4,1,0,3:T(8,128)(2,1)S(1)} %get-tuple-element.19, bf16[2,1,16,4,2,256]{5,2,4,1,0,3:T(8,128)(2,1)S(1)} %get-tuple-element.18), kind=kOutput, calls=%fused_computation.33 | convolution fusion | flops 403963904 | bytes 13680640 | tf_op jit(solution)/shard_map/jfavcs,ijfkcs->ijfavk/dot_general | solution.py:55
  19.4 1.7 copy.96
  21.1 8.4 %all-to-all-start = ((bf16[16,4,2,2,1536]{4,3,2,1,0:T(2,128)(2,1)}), bf16[16,4,2,2,1536]{4,3,2,1,0:T(2,128)(2,1)S(1)}, u32[]{:S(2)}, u32[]{:S(2)}) async-start(bf16[16,4,2,2,1536]{4,3,2,1,0:T(2,128)(2,1)} %copy.96), calls=%async_computation | async-start | bytes 1572864 | tf_op jit(solution)/shard_map/all_to_all | solution.py:60
  29.7 14.3 %all-to-all-done = bf16[16,4,2,2,1536]{4,3,2,1,0:T(2,128)(2,1)S(1)} async-done(((bf16[16,4,2,2,1536]{4,3,2,1,0:T(2,128)(2,1)}), bf16[16,4,2,2,1536]{4,3,2,1,0:T(2,128)(2,1)S(1)}, u32[]{:S(2)}, u32[]{:S(2)}) %all-to-all-start) | async-done | bytes 786464 | tf_op jit(solution)/shard_map/all_to_all | solution.py:60
  45.2 6.9 %fusion.47 = f32[1,2,2,16,2,256]{5,3,4,2,1,0:T(8,128)S(1)} fusion(bf16[64,2,96,2,256,1]{4,3,2,1,0,5:T(2,128)(2,1)} %bitcast.353, bf16[64,2,2,16,96,1]{4,3,0,2,1,5:T(8,128)(2,1)S(1)} %reshape.457), kind=kOutput, calls=%fused_computation.40 | convolution fusion | flops 402653184 | bytes 13500416 | tf_op jit(solution)/shard_map/ijfavk,ijfkcn->ifavcn/dot_general | solution.py:62
  54.1 7.6 %fusion.35 = bf16[1,64,2,2,16,96]{5,4,1,3,2,0:T(8,128)(2,1)S(1)} fusion(bf16[64,2,96,2,256,1]{4,3,2,1,0,5:T(2,128)(2,1)} %bitcast.354, bf16[2,1,16,1,2,256]{5,2,4,1,0,3:T(8,128)(2,1)S(1)} %get-tuple-element.29, bf16[2,1,16,1,2,256]{5,2,4,1,0,3:T(8,128)(2,1)S(1)} %get-tuple-element.28), kind=kOutput, calls=%fused_computation.36 | convolution fusion | flops 403177472 | bytes 13434880 | tf_op jit(solution)/shard_map/ifavcn,ijfkcn->ijfavk/dot_general | solution.py:71
  63.0 1.7 copy.106
  64.7 3.6 %all-to-all-start.1 = ((bf16[1,64,2,2,1536]{4,3,2,0,1:T(2,128)(2,1)}), bf16[1,64,2,2,1536]{4,3,2,0,1:T(2,128)(2,1)S(1)}, u32[]{:S(2)}, u32[]{:S(2)}) async-start(bf16[1,64,2,2,1536]{4,3,2,0,1:T(2,128)(2,1)} %copy.106), calls=%async_computation.1 | async-start | bytes 1572864 | tf_op jit(solution)/shard_map/all_to_all | solution.py:76
  69.0 12.5 %all-to-all-done.1 = bf16[1,64,2,2,1536]{4,3,2,0,1:T(2,128)(2,1)S(1)} async-done(((bf16[1,64,2,2,1536]{4,3,2,0,1:T(2,128)(2,1)}), bf16[1,64,2,2,1536]{4,3,2,0,1:T(2,128)(2,1)S(1)}, u32[]{:S(2)}, u32[]{:S(2)}) %all-to-all-start.1) | async-done | bytes 786464 | tf_op jit(solution)/shard_map/all_to_all | solution.py:76
  82.5 6.9 %fusion.41 = f32[4,2,2,16,2,256]{5,3,4,2,1,0:T(8,128)S(1)} fusion(bf16[16,4,2,96,2,256,1]{5,4,3,2,1,0,6:T(2,128)(2,1)} %bitcast.385, bf16[16,4,2,2,16,96]{5,4,1,0,3,2:T(8,128)(2,1)S(1)} %reshape.443, bf16[16,4,2,96]{3,1,0,2:T(4,128)(2,1)S(1)} %copy.108), kind=kOutput, calls=%fused_computation.38 | convolution fusion | flops 403046400 | bytes 13918208 | tf_op jit(solution)/shard_map/ijfavk,ijfkcs->jfavcs/dot_general | solution.py:79
  90.2 55.2 %all-reduce.3.cloned.1.call-done = bf16[2,2,16,1024]{3,2,1,0:T(8,128)(2,1)} async-done(((bf16[2,2,16,1024]{3,2,1,0:T(8,128)(2,1)}), bf16[2,2,16,1024]{3,2,1,0:T(8,128)(2,1)}) %all-reduce.3.cloned.1.call-update) | async-done | bytes 131088 | tf_op jit(solution)/shard_map/psum | solution.py:94
  146.6 9.1 %fusion.23 = bf16[16,4,2,2,16,96]{5,4,0,3,2,1:T(8,128)(2,1)S(1)} fusion(bf16[16,4,2,96,2,256,1]{5,4,3,2,1,0,6:T(2,128)(2,1)} %bitcast.386, f32[16,4,2,96]{3,0,2,1:T(8,128)S(1)} %get-tuple-element.31, bf16[2,1,16,4,2,256]{5,2,4,1,0,3:T(8,128)(2,1)S(1)} %get-tuple-element.15, bf16[2,1,16,4,2,256]{5,2,4,1,0,3:T(8,128)(2,1)S(1)} %get-tuple-element.14), kind=kOutput, calls=%fused_computation.31 | convolution fusion | flops 403963904 | bytes 13680640 | tf_op jit(solution)/shard_map/jfavcs,ijfkcs->ijfavk/dot_general | solution.py:55
  157.7 22.1 %all_to_all.20 = bf16[16,4,2,2,1536]{4,3,2,1,0:T(2,128)(2,1)S(1)} all-to-all(bf16[16,4,2,2,1536]{4,3,2,1,0:T(2,128)(2,1)S(1)} %copy.119), channel_id=1, replica_groups=mesh['row'=8,'col'=16] {'col'}, dimensions={0} | all-to-all | bytes 1572864 | tf_op jit(solution)/shard_map/all_to_all | solution.py:60
  181.0 6.9 %fusion.50 = f32[1,2,2,16,2,256]{5,3,4,2,1,0:T(8,128)S(1)} fusion(bf16[64,2,96,2,256,1]{4,3,2,1,0,5:T(2,128)(2,1)} %bitcast.355, bf16[64,2,2,16,96,1]{4,3,0,2,1,5:T(8,128)(2,1)S(1)} %reshape.469), kind=kOutput, calls=%fused_computation.41 | convolution fusion | flops 402653184 | bytes 13500416 | tf_op jit(solution)/shard_map/ijfavk,ijfkcn->ifavcn/dot_general | solution.py:62
  188.0 1.2 convolution_select_fusion.1
  189.9 7.6 %fusion.38 = bf16[1,64,2,2,16,96]{5,4,1,3,2,0:T(8,128)(2,1)S(1)} fusion(bf16[64,2,96,2,256,1]{4,3,2,1,0,5:T(2,128)(2,1)} %bitcast.356, bf16[2,1,16,1,2,256]{5,2,4,1,0,3:T(8,128)(2,1)S(1)} %get-tuple-element.27, bf16[2,1,16,1,2,256]{5,2,4,1,0,3:T(8,128)(2,1)S(1)} %get-tuple-element.26), kind=kOutput, calls=%fused_computation.37 | convolution fusion | flops 403177472 | bytes 13434880 | tf_op jit(solution)/shard_map/ifavcn,ijfkcn->ijfavk/dot_general | solution.py:71
  199.6 17.2 %all_to_all.21 = bf16[1,64,2,2,1536]{4,3,2,0,1:T(2,128)(2,1)S(1)} all-to-all(bf16[1,64,2,2,1536]{4,3,2,0,1:T(2,128)(2,1)S(1)} %copy.129), channel_id=1, replica_groups=mesh['row'=8,'col'=16] {'col'}, dimensions={1} | all-to-all | bytes 1572864 | tf_op jit(solution)/shard_map/all_to_all | solution.py:76
  217.8 6.9 %fusion.44 = f32[4,2,2,16,2,256]{5,3,4,2,1,0:T(8,128)S(1)} fusion(bf16[16,4,2,96,2,256,1]{5,4,3,2,1,0,6:T(2,128)(2,1)} %bitcast.387, bf16[16,4,2,2,16,96]{5,4,1,0,3,2:T(8,128)(2,1)S(1)} %reshape.449, bf16[16,4,2,96]{3,1,0,2:T(4,128)(2,1)S(1)} %copy.108), kind=kOutput, calls=%fused_computation.39 | convolution fusion | flops 403046400 | bytes 13918208 | tf_op jit(solution)/shard_map/ijfavk,ijfkcs->jfavcs/dot_general | solution.py:79
  225.5 54.9 %all-reduce.5.cloned.1.call-done = bf16[2,2,16,1024]{3,2,1,0:T(8,128)(2,1)} async-done(((bf16[2,2,16,1024]{3,2,1,0:T(8,128)(2,1)}), bf16[2,2,16,1024]{3,2,1,0:T(8,128)(2,1)}) %all-reduce.5.cloned.1.call-update) | async-done | bytes 131088 | tf_op jit(solution)/shard_map/psum | solution.py:94
  280.3 1.7 fusion.105
  282.2 9.1 %fusion.22 = bf16[16,4,2,2,16,96]{5,4,0,3,2,1:T(8,128)(2,1)S(1)} fusion(bf16[16,4,2,96,2,256,1]{5,4,3,2,1,0,6:T(2,128)(2,1)} %bitcast.388, f32[16,4,2,96]{3,0,2,1:T(8,128)S(1)} %get-tuple-element.31, bf16[2,1,16,4,2,256]{5,2,4,1,0,3:T(8,128)(2,1)S(1)} %get-tuple-element.11, bf16[2,1,16,4,2,256]{5,2,4,1,0,3:T(8,128)(2,1)S(1)} %get-tuple-element.10), kind=kOutput, calls=%fused_computation.29 | convolution fusion | flops 403963904 | bytes 13680640 | tf_op jit(solution)/shard_map/jfavcs,ijfkcs->ijfavk/dot_general | solution.py:55
  293.3 22.2 %all_to_all.22 = bf16[16,4,2,2,1536]{4,3,2,1,0:T(2,128)(2,1)S(1)} all-to-all(bf16[16,4,2,2,1536]{4,3,2,1,0:T(2,128)(2,1)S(1)} %copy.141), channel_id=1, replica_groups=mesh['row'=8,'col'=16] {'col'}, dimensions={0} | all-to-all | bytes 1572864 | tf_op jit(solution)/shard_map/all_to_all | solution.py:60
  316.7 6.9 %fusion.53 = f32[1,2,2,16,2,256]{5,3,4,2,1,0:T(8,128)S(1)} fusion(bf16[64,2,96,2,256,1]{4,3,2,1,0,5:T(2,128)(2,1)} %bitcast.357, bf16[64,2,2,16,96,1]{4,3,0,2,1,5:T(8,128)(2,1)S(1)} %reshape.481), kind=kOutput, calls=%fused_computation.42 | convolution fusion | flops 402653184 | bytes 13500416 | tf_op jit(solution)/shard_map/ijfavk,ijfkcn->ifavcn/dot_general | solution.py:62
  323.7 1.2 convolution_select_fusion
  (93 shorter events, 23.6 us)
Async XLA Ops:
  7.2 22.3 %copy-start.3 = (s32[16,256]{1,0:T(8,128)S(1)}, s32[16,256]{1,0:T(8,128)}, u32[]{:S(2)}) copy-start(s32[16,256]{1,0:T(8,128)} %param.12) | copy-start | bytes 49156
  7.2 22.4 %copy-start.4 = (s32[16,256]{1,0:T(8,128)S(1)}, s32[16,256]{1,0:T(8,128)}, u32[]{:S(2)}) copy-start(s32[16,256]{1,0:T(8,128)} %param.13) | copy-start | bytes 49156
  18.2 33.9 %copy-start.1 = (f32[2,2,16,256]{3,2,1,0:T(8,128)S(1)}, f32[2,2,16,256]{3,2,1,0:T(8,128)}, u32[]{:S(2)}) copy-start(f32[2,2,16,256]{3,2,1,0:T(8,128)} %param.8) | copy-start | bytes 196612
  21.1 22.9 %all-to-all-start = ((bf16[16,4,2,2,1536]{4,3,2,1,0:T(2,128)(2,1)}), bf16[16,4,2,2,1536]{4,3,2,1,0:T(2,128)(2,1)S(1)}, u32[]{:S(2)}, u32[]{:S(2)}) async-start(bf16[16,4,2,2,1536]{4,3,2,1,0:T(2,128)(2,1)} %copy.96), calls=%async_computation | async-start | bytes 1572864 | tf_op jit(solution)/shard_map/all_to_all | solution.py:60
  61.8 83.7 %copy-start = (f32[2,2,16,1024]{3,2,1,0:T(8,128)S(1)}, f32[2,2,16,1024]{3,2,1,0:T(8,128)}, u32[]{:S(2)}) copy-start(f32[2,2,16,1024]{3,2,1,0:T(8,128)} %param.7) | copy-start | bytes 786436
  64.7 16.8 %all-to-all-start.1 = ((bf16[1,64,2,2,1536]{4,3,2,0,1:T(2,128)(2,1)}), bf16[1,64,2,2,1536]{4,3,2,0,1:T(2,128)(2,1)S(1)}, u32[]{:S(2)}, u32[]{:S(2)}) async-start(bf16[1,64,2,2,1536]{4,3,2,0,1:T(2,128)(2,1)} %copy.106), calls=%async_computation.1 | async-start | bytes 1572864 | tf_op jit(solution)/shard_map/all_to_all | solution.py:76
  68.3 77.1 %all-reduce.3.cloned.1.call-start = ((), (), s32[]{:S(2)}) async-start(), calls=%async_computation.5 | async-start | bytes 262144 | tf_op jit(solution)/shard_map/psum | solution.py:94
  90.2 190.2 %all-reduce.5.cloned.1.call-start = ((), (), s32[]{:S(2)}) async-start(), calls=%async_computation.6 | async-start | bytes 262144 | tf_op jit(solution)/shard_map/psum | solution.py:94
  197.5 82.8 %copy-start.2 = (bf16[2,2,16,1024]{3,2,1,0:T(8,128)(2,1)S(1)}, bf16[2,2,16,1024]{3,2,1,0:T(8,128)(2,1)}, u32[]{:S(2)}) copy-start(bf16[2,2,16,1024]{3,2,1,0:T(8,128)(2,1)} %all-reduce.3.cloned.1.call-done) | copy-start | bytes 393220
Sparse Core Ops, SparseCore 0:
  90.3 55.1 all-reduce.2
  225.6 54.6 all-reduce.4
where the time goes:
time: 338 us; the launch traced here: 333 us
  waiting for transfers between devices  137 us (41%)
  matrix products  82.3 us (24%)
  blocking collectives  61.5 us (18%)
  local copies, waits for them, and re-layouts  20.1 us (6%)
  between operations  14.9 us (4%)
  starting transfers between devices  12.7 us (4%)
  other arithmetic  4.85 us (1%)
    psum x2, waiting for transfers between devices, shards(): lax.psum(grad_local.astype(jnp.bfloat16), 'row').astype(jnp.float32)  110 us
    all_to_all x2, blocking collectives, forward(): lax.all_to_all(sendable, 'col', split_axis=0, concat_axis=1, tiled=True)  44.3 us
    dot_general x3, matrix products, forward(): jnp.einsum('jfavcs,ijfkcs->ijfavk', paired, right_bases, preferred_elemen...  27.3 us
    dot_general x3, matrix products, forward(): jnp.einsum('ijfavk,ijfkcn->ifavcn', received, left_bases, preferred_eleme...  20.6 us
    all_to_all x1, blocking collectives, adjoint(): lax.all_to_all(sendable, 'col', split_axis=1, concat_axis=0, tiled=True)  17.2 us
    dot_general x2, matrix products, adjoint(): jnp.einsum('ifavcn,ijfkcn->ijfavk', paired, left_bases, preferred_element...  15.2 us
    all_to_all x1, waiting for transfers between devices, forward(): lax.all_to_all(sendable, 'col', split_axis=0, concat_axis=1, tiled=True)  14.3 us
    dot_general x2, matrix products, adjoint(): jnp.einsum('ijfavk,ijfkcs->jfavcs', received, right_bases, preferred_elem...  13.8 us
  transfers between devices with their start and end apart: 4, of which 4 were waited for; matrix products, arithmetic and copies ran while one was open for 0% of the time, Pallas kernels for 0%

commit v1 on v0

--- a/solution.py
+++ b/solution.py
@@ -91,7 +91,9 @@
         predicted = forward(low_model, left_bases, right_bases, rank_keep)
         residual = apply_gate(predicted - observed, gate_start, gate_stop)
         grad_local = adjoint(residual, left_bases, right_bases, rank_keep)
-        gradient = lax.psum(grad_local.astype(jnp.bfloat16), "row").astype(jnp.float32)
+        gradient = jnp.sum(lax.all_gather(grad_local.astype(jnp.bfloat16), "row"), axis=0).astype(
+            jnp.float32
+        )
         estimate = estimate - step_length * gradient
         low_model = estimate.astype(jnp.bfloat16)
     predicted = forward(low_model, left_bases, right_bases, rank_keep)

time: 338 us -> 270 us (0.80)
  the two profiles are of different devices: /device:TPU:6 before, /device:TPU:1 now
where the time goes in v1:
time: 270 us; the launch traced here: 265 us
  matrix products  82.3 us (30%)
  waiting for transfers between devices  70 us (26%)
  blocking collectives  57.9 us (21%)
  local copies, waits for them, and re-layouts  20.4 us (8%)
  between operations  15.2 us (6%)
  starting transfers between devices  13.1 us (5%)
  other arithmetic  5.85 us (2%)
    all_gather x2, waiting for transfers between devices, shards(): lax.all_gather(grad_local.astype(jnp.bfloat16), 'row')  44.7 us
    all_to_all x2, blocking collectives, forward(): lax.all_to_all(sendable, 'col', split_axis=0, concat_axis=1, tiled=True)  41.3 us
    dot_general x3, matrix products, forward(): jnp.einsum('jfavcs,ijfkcs->ijfavk', paired, right_bases, preferred_elemen...  27.3 us
    dot_general x3, matrix products, forward(): jnp.einsum('ijfavk,ijfkcn->ifavcn', received, left_bases, preferred_eleme...  20.6 us
    all_to_all x1, blocking collectives, adjoint(): lax.all_to_all(sendable, 'col', split_axis=1, concat_axis=0, tiled=True)  16.5 us
    dot_general x2, matrix products, adjoint(): jnp.einsum('ifavcn,ijfkcn->ijfavk', paired, left_bases, preferred_element...  15.2 us
    dot_general x2, matrix products, adjoint(): jnp.einsum('ijfavk,ijfkcs->jfavcs', received, right_bases, preferred_elem...  13.8 us
    all_to_all x1, waiting for transfers between devices, forward(): lax.all_to_all(sendable, 'col', split_axis=0, concat_axis=1, tiled=True)  13 us
  transfers between devices with their start and end apart: 4, of which 4 were waited for; matrix products, arithmetic and copies ran while one was open for 0% of the time, Pallas kernels for 0%

profile of v1, /device:TPU:1, one launch (start us, length us, event | category | flops | bytes accessed | tf_op | source)
XLA Modules:
  0.0 264.6 jit_solution(7006855825519075777)
XLA Ops:
  9.1 9.1 %fusion.24 = bf16[16,4,2,2,16,96]{5,4,0,3,2,1:T(8,128)(2,1)S(1)} fusion(bf16[16,4,2,96,2,256,1]{5,4,3,2,1,0,6:T(2,128)(2,1)} %bitcast.378, f32[16,4,2,96]{3,0,2,1:T(8,128)S(1)} %get-tuple-element.31, bf16[2,1,16,4,2,256]{5,2,4,1,0,3:T(8,128)(2,1)S(1)} %get-tuple-element.19, bf16[2,1,16,4,2,256]{5,2,4,1,0,3:T(8,128)(2,1)S(1)} %get-tuple-element.18), kind=kOutput, calls=%fused_computation.33 | convolution fusion | flops 403963904 | bytes 13680640 | tf_op jit(solution)/shard_map/jfavcs,ijfkcs->ijfavk/dot_general | solution.py:55
  19.4 1.7 copy.96
  21.1 9.1 %all-to-all-start = ((bf16[16,4,2,2,1536]{4,3,2,1,0:T(2,128)(2,1)}), bf16[16,4,2,2,1536]{4,3,2,1,0:T(2,128)(2,1)S(1)}, u32[]{:S(2)}, u32[]{:S(2)}) async-start(bf16[16,4,2,2,1536]{4,3,2,1,0:T(2,128)(2,1)} %copy.96), calls=%async_computation | async-start | bytes 1572864 | tf_op jit(solution)/shard_map/all_to_all | solution.py:60
  30.4 13.0 %all-to-all-done = bf16[16,4,2,2,1536]{4,3,2,1,0:T(2,128)(2,1)S(1)} async-done(((bf16[16,4,2,2,1536]{4,3,2,1,0:T(2,128)(2,1)}), bf16[16,4,2,2,1536]{4,3,2,1,0:T(2,128)(2,1)S(1)}, u32[]{:S(2)}, u32[]{:S(2)}) %all-to-all-start) | async-done | bytes 786464 | tf_op jit(solution)/shard_map/all_to_all | solution.py:60
  44.7 6.9 %fusion.47 = f32[1,2,2,16,2,256]{5,3,4,2,1,0:T(8,128)S(1)} fusion(bf16[64,2,96,2,256,1]{4,3,2,1,0,5:T(2,128)(2,1)} %bitcast.349, bf16[64,2,2,16,96,1]{4,3,0,2,1,5:T(8,128)(2,1)S(1)} %reshape.477), kind=kOutput, calls=%fused_computation.40 | convolution fusion | flops 402653184 | bytes 13500416 | tf_op jit(solution)/shard_map/ijfavk,ijfkcn->ifavcn/dot_general | solution.py:62
  53.6 7.6 %fusion.35 = bf16[1,64,2,2,16,96]{5,4,1,3,2,0:T(8,128)(2,1)S(1)} fusion(bf16[64,2,96,2,256,1]{4,3,2,1,0,5:T(2,128)(2,1)} %bitcast.350, bf16[2,1,16,1,2,256]{5,2,4,1,0,3:T(8,128)(2,1)S(1)} %get-tuple-element.29, bf16[2,1,16,1,2,256]{5,2,4,1,0,3:T(8,128)(2,1)S(1)} %get-tuple-element.28), kind=kOutput, calls=%fused_computation.36 | convolution fusion | flops 403177472 | bytes 13434880 | tf_op jit(solution)/shard_map/ifavcn,ijfkcn->ijfavk/dot_general | solution.py:71
  62.4 1.7 copy.106
  64.1 3.7 %all-to-all-start.1 = ((bf16[1,64,2,2,1536]{4,3,2,0,1:T(2,128)(2,1)}), bf16[1,64,2,2,1536]{4,3,2,0,1:T(2,128)(2,1)S(1)}, u32[]{:S(2)}, u32[]{:S(2)}) async-start(bf16[1,64,2,2,1536]{4,3,2,0,1:T(2,128)(2,1)} %copy.106), calls=%async_computation.1 | async-start | bytes 1572864 | tf_op jit(solution)/shard_map/all_to_all | solution.py:76
  68.1 12.2 %all-to-all-done.1 = bf16[1,64,2,2,1536]{4,3,2,0,1:T(2,128)(2,1)S(1)} async-done(((bf16[1,64,2,2,1536]{4,3,2,0,1:T(2,128)(2,1)}), bf16[1,64,2,2,1536]{4,3,2,0,1:T(2,128)(2,1)S(1)}, u32[]{:S(2)}, u32[]{:S(2)}) %all-to-all-start.1) | async-done | bytes 786464 | tf_op jit(solution)/shard_map/all_to_all | solution.py:76
  81.2 6.9 %fusion.41 = f32[4,2,2,16,2,256]{5,3,4,2,1,0:T(8,128)S(1)} fusion(bf16[16,4,2,96,2,256,1]{5,4,3,2,1,0,6:T(2,128)(2,1)} %bitcast.379, bf16[16,4,2,2,16,96]{5,4,1,0,3,2:T(8,128)(2,1)S(1)} %reshape.463, bf16[16,4,2,96]{3,1,0,2:T(4,128)(2,1)S(1)} %copy.108), kind=kOutput, calls=%fused_computation.38 | convolution fusion | flops 403046400 | bytes 13918208 | tf_op jit(solution)/shard_map/ijfavk,ijfkcs->jfavcs/dot_general | solution.py:79
  89.1 23.6 %all-gather.3.cloned.1.call-done = bf16[8,2,2,16,1024]{4,3,2,1,0:T(8,128)(2,1)} async-done(((bf16[1,2,2,16,1024]{4,3,2,1,0:T(8,128)(2,1)}), bf16[8,2,2,16,1024]{4,3,2,1,0:T(8,128)(2,1)}) %all-gather.3.cloned.1.call-update) | async-done | bytes 1048592 | tf_op jit(solution)/shard_map/all_gather | solution.py:94
  112.7 1.4 reduce_sum.24
  114.3 9.1 %fusion.23 = bf16[16,4,2,2,16,96]{5,4,0,3,2,1:T(8,128)(2,1)S(1)} fusion(bf16[16,4,2,96,2,256,1]{5,4,3,2,1,0,6:T(2,128)(2,1)} %bitcast.380, f32[16,4,2,96]{3,0,2,1:T(8,128)S(1)} %get-tuple-element.31, bf16[2,1,16,4,2,256]{5,2,4,1,0,3:T(8,128)(2,1)S(1)} %get-tuple-element.15, bf16[2,1,16,4,2,256]{5,2,4,1,0,3:T(8,128)(2,1)S(1)} %get-tuple-element.14), kind=kOutput, calls=%fused_computation.31 | convolution fusion | flops 403963904 | bytes 13680640 | tf_op jit(solution)/shard_map/jfavcs,ijfkcs->ijfavk/dot_general | solution.py:55
  125.5 20.6 %all_to_all.20 = bf16[16,4,2,2,1536]{4,3,2,1,0:T(2,128)(2,1)S(1)} all-to-all(bf16[16,4,2,2,1536]{4,3,2,1,0:T(2,128)(2,1)S(1)} %copy.119), channel_id=1, replica_groups=mesh['row'=8,'col'=16] {'col'}, dimensions={0} | all-to-all | bytes 1572864 | tf_op jit(solution)/shard_map/all_to_all | solution.py:60
  147.3 6.9 %fusion.50 = f32[1,2,2,16,2,256]{5,3,4,2,1,0:T(8,128)S(1)} fusion(bf16[64,2,96,2,256,1]{4,3,2,1,0,5:T(2,128)(2,1)} %bitcast.351, bf16[64,2,2,16,96,1]{4,3,0,2,1,5:T(8,128)(2,1)S(1)} %reshape.489), kind=kOutput, calls=%fused_computation.41 | convolution fusion | flops 402653184 | bytes 13500416 | tf_op jit(solution)/shard_map/ijfavk,ijfkcn->ifavcn/dot_general | solution.py:62
  156.2 7.6 %fusion.38 = bf16[1,64,2,2,16,96]{5,4,1,3,2,0:T(8,128)(2,1)S(1)} fusion(bf16[64,2,96,2,256,1]{4,3,2,1,0,5:T(2,128)(2,1)} %bitcast.352, bf16[2,1,16,1,2,256]{5,2,4,1,0,3:T(8,128)(2,1)S(1)} %get-tuple-element.27, bf16[2,1,16,1,2,256]{5,2,4,1,0,3:T(8,128)(2,1)S(1)} %get-tuple-element.26), kind=kOutput, calls=%fused_computation.37 | convolution fusion | flops 403177472 | bytes 13434880 | tf_op jit(solution)/shard_map/ifavcn,ijfkcn->ijfavk/dot_general | solution.py:71
  165.9 16.5 %all_to_all.21 = bf16[1,64,2,2,1536]{4,3,2,0,1:T(2,128)(2,1)S(1)} all-to-all(bf16[1,64,2,2,1536]{4,3,2,0,1:T(2,128)(2,1)S(1)} %copy.129), channel_id=1, replica_groups=mesh['row'=8,'col'=16] {'col'}, dimensions={1} | all-to-all | bytes 1572864 | tf_op jit(solution)/shard_map/all_to_all | solution.py:76
  183.4 6.9 %fusion.44 = f32[4,2,2,16,2,256]{5,3,4,2,1,0:T(8,128)S(1)} fusion(bf16[16,4,2,96,2,256,1]{5,4,3,2,1,0,6:T(2,128)(2,1)} %bitcast.381, bf16[16,4,2,2,16,96]{5,4,1,0,3,2:T(8,128)(2,1)S(1)} %reshape.469, bf16[16,4,2,96]{3,1,0,2:T(4,128)(2,1)S(1)} %copy.108), kind=kOutput, calls=%fused_computation.39 | convolution fusion | flops 403046400 | bytes 13918208 | tf_op jit(solution)/shard_map/ijfavk,ijfkcs->jfavcs/dot_general | solution.py:79
  191.2 21.2 %all-gather.5.cloned.1.call-done = bf16[8,2,2,16,1024]{4,3,2,1,0:T(8,128)(2,1)} async-done(((bf16[1,2,2,16,1024]{4,3,2,1,0:T(8,128)(2,1)}), bf16[8,2,2,16,1024]{4,3,2,1,0:T(8,128)(2,1)}) %all-gather.5.cloned.1.call-update) | async-done | bytes 1048592 | tf_op jit(solution)/shard_map/all_gather | solution.py:94
  212.4 1.4 reduce_sum.25
  214.8 9.1 %fusion.22 = bf16[16,4,2,2,16,96]{5,4,0,3,2,1:T(8,128)(2,1)S(1)} fusion(bf16[16,4,2,96,2,256,1]{5,4,3,2,1,0,6:T(2,128)(2,1)} %bitcast.382, f32[16,4,2,96]{3,0,2,1:T(8,128)S(1)} %get-tuple-element.31, bf16[2,1,16,4,2,256]{5,2,4,1,0,3:T(8,128)(2,1)S(1)} %get-tuple-element.11, bf16[2,1,16,4,2,256]{5,2,4,1,0,3:T(8,128)(2,1)S(1)} %get-tuple-element.10), kind=kOutput, calls=%fused_computation.29 | convolution fusion | flops 403963904 | bytes 13680640 | tf_op jit(solution)/shard_map/jfavcs,ijfkcs->ijfavk/dot_general | solution.py:55
  225.9 20.7 %all_to_all.22 = bf16[16,4,2,2,1536]{4,3,2,1,0:T(2,128)(2,1)S(1)} all-to-all(bf16[16,4,2,2,1536]{4,3,2,1,0:T(2,128)(2,1)S(1)} %copy.141), channel_id=1, replica_groups=mesh['row'=8,'col'=16] {'col'}, dimensions={0} | all-to-all | bytes 1572864 | tf_op jit(solution)/shard_map/all_to_all | solution.py:60
  247.8 6.9 %fusion.53 = f32[1,2,2,16,2,256]{5,3,4,2,1,0:T(8,128)S(1)} fusion(bf16[64,2,96,2,256,1]{4,3,2,1,0,5:T(2,128)(2,1)} %bitcast.353, bf16[64,2,2,16,96,1]{4,3,0,2,1,5:T(8,128)(2,1)S(1)} %reshape.501), kind=kOutput, calls=%fused_computation.42 | convolution fusion | flops 402653184 | bytes 13500416 | tf_op jit(solution)/shard_map/ijfavk,ijfkcn->ifavcn/dot_general | solution.py:62
  254.8 1.2 convolution_select_fusion
  (95 shorter events, 24.6 us)
Async XLA Ops:
  7.2 23.1 %copy-start.2 = (s32[16,256]{1,0:T(8,128)S(1)}, s32[16,256]{1,0:T(8,128)}, u32[]{:S(2)}) copy-start(s32[16,256]{1,0:T(8,128)} %param.12) | copy-start | bytes 49156
  7.2 23.1 %copy-start.3 = (s32[16,256]{1,0:T(8,128)S(1)}, s32[16,256]{1,0:T(8,128)}, u32[]{:S(2)}) copy-start(s32[16,256]{1,0:T(8,128)} %param.13) | copy-start | bytes 49156
  18.2 33.4 %copy-start.1 = (f32[2,2,16,256]{3,2,1,0:T(8,128)S(1)}, f32[2,2,16,256]{3,2,1,0:T(8,128)}, u32[]{:S(2)}) copy-start(f32[2,2,16,256]{3,2,1,0:T(8,128)} %param.8) | copy-start | bytes 196612
  21.1 22.3 %all-to-all-start = ((bf16[16,4,2,2,1536]{4,3,2,1,0:T(2,128)(2,1)}), bf16[16,4,2,2,1536]{4,3,2,1,0:T(2,128)(2,1)S(1)}, u32[]{:S(2)}, u32[]{:S(2)}) async-start(bf16[16,4,2,2,1536]{4,3,2,1,0:T(2,128)(2,1)} %copy.96), calls=%async_computation | async-start | bytes 1572864 | tf_op jit(solution)/shard_map/all_to_all | solution.py:60
  62.4 51.7 %copy-start = (f32[2,2,16,1024]{3,2,1,0:T(8,128)S(1)}, f32[2,2,16,1024]{3,2,1,0:T(8,128)}, u32[]{:S(2)}) copy-start(f32[2,2,16,1024]{3,2,1,0:T(8,128)} %param.7) | copy-start | bytes 786436
  64.1 16.1 %all-to-all-start.1 = ((bf16[1,64,2,2,1536]{4,3,2,0,1:T(2,128)(2,1)}), bf16[1,64,2,2,1536]{4,3,2,0,1:T(2,128)(2,1)S(1)}, u32[]{:S(2)}, u32[]{:S(2)}) async-start(bf16[1,64,2,2,1536]{4,3,2,0,1:T(2,128)(2,1)} %copy.106), calls=%async_computation.1 | async-start | bytes 1572864 | tf_op jit(solution)/shard_map/all_to_all | solution.py:76
  67.8 44.9 %all-gather.3.cloned.1.call-start = ((), (), s32[]{:S(2)}) async-start(), calls=%async_computation.5 | async-start | bytes 1179648 | tf_op jit(solution)/shard_map/all_gather | solution.py:94
  89.1 123.3 %all-gather.5.cloned.1.call-start = ((), (), s32[]{:S(2)}) async-start(), calls=%async_computation.6 | async-start | bytes 1179648 | tf_op jit(solution)/shard_map/all_gather | solution.py:94
Sparse Core Ops, SparseCore 0:
  89.2 23.4 all-gather.2
  191.3 21.0 all-gather.4
